TPU v7x, 32 devices: a whole 2x2x4 slice. The times are simulated.
32 devices in a mesh: row: 8 (over y, x, core), ctx: 4 (over z).
Axes of the slice: x: 2, y: 2, z: 4, core: 2. Of those that a mesh axis runs over, the one named last changes fastest.
Arguments:
- queries: bfloat16 [5, 4096, 128], P(None, ('row', 'ctx')), may hold values from -100 to 100
- keys: bfloat16 [4096, 128], P('ctx'), may hold values from -6 to 6
- doc_ids: int32 [64], replicated, may hold values from 0 to 3, never falling along the last dimension, each value on 1 to 48 neighbouring positions
- gate_query: bfloat16 [5, 128, 128], replicated, may hold values from -0.5 to 0.5
- gate_key: bfloat16 [384, 128], replicated, may hold values from -0.3125 to 0.3125
Outputs:
- block_map: float32 [5, 64, 64], P(None, ('row', 'ctx'))
- grad_query: float32 [5, 128, 128], replicated
- grad_key: float32 [384, 128], replicated
Inputs may be any that keep to these rules, and one draw needn't show every extreme that they name: `doc_ids`: block document ids never fall along the sequence; each document spans 1 to 48 blocks and one spans exactly 48.
All inputs are finite; a program needn't handle non-finite values.
Results may differ from a plain program's by a relative error of at most 0.0003.
Values may be sent and summed in bfloat16 or wider, within the bound.
A program may use at most 64 MiB of HBM per device.

v0:
```python
import math
import jax
import jax.numpy as jnp
from jax import lax
from jax.sharding import PartitionSpec as P

BLK = 64
NEG_FILL = -1e30
BLOCK_CAP = 512


def pool_keys(key_block, block_len):
    grouped = key_block.astype(jnp.float32).reshape(
        key_block.shape[0] // block_len, block_len, key_block.shape[1]
    )
    return jnp.concatenate(
        [jnp.max(grouped, axis=1), jnp.min(grouped, axis=1), jnp.mean(grouped, axis=1)], axis=1
    )


def held_positions(row_index, ctx_index, ctx_total, row_count):
    half_rows = row_count // 2
    home_start = (row_index * ctx_total + ctx_index) * row_count
    far_start = home_start + half_rows
    offsets = jnp.arange(half_rows, dtype=jnp.int32)
    return jnp.concatenate([home_start + offsets, far_start + offsets])


def block_docs(doc_ids, positions, block_len):
    block_starts = positions.reshape(-1, block_len)[:, 0] // block_len
    return jnp.repeat(jnp.take(doc_ids, block_starts), block_len)


def tile_update(
    carried,
    held_rows,
    query_pos,
    query_doc,
    key_block,
    key_start,
    table_base,
    doc_ids,
    block_len,
    score_scale,
):
    score_table, row_max, row_sum = carried
    key_count = key_block.shape[0]
    head_count, row_count = (held_rows.shape[0], held_rows.shape[1])
    scores = (
        jnp.einsum("hrd,kd->hrk", held_rows, key_block, preferred_element_type=jnp.float32)
        * score_scale
    )
    key_pos = key_start + jnp.arange(key_count, dtype=jnp.int32)
    key_doc = jnp.repeat(
        lax.dynamic_slice_in_dim(doc_ids, key_start // block_len, key_count // block_len), block_len
    )
    allowed = (key_pos[None, :] <= query_pos[:, None]) & (key_doc[None, :] == query_doc[:, None])
    masked = jnp.where(allowed[None], scores, NEG_FILL)
    block_peaks = jnp.max(
        masked.reshape(head_count, row_count, key_count // block_len, block_len), axis=3
    )
    score_table = lax.dynamic_update_slice_in_dim(
        score_table, block_peaks, (key_start - table_base) // block_len, 2
    )
    new_max = jnp.maximum(row_max, jnp.max(masked, axis=2))
    weights = jnp.where(allowed[None], jnp.exp(masked - new_max[:, :, None]), 0.0)
    row_sum = row_sum * jnp.exp(row_max - new_max) + jnp.sum(weights, axis=2)
    return (score_table, new_max, row_sum)


def finish_maps(score_table, row_max, row_sum, block_len):
    log_total = row_max + jnp.log(row_sum)
    chances = jnp.exp(score_table - log_total[:, :, None])
    head_count, row_count, column_count = chances.shape
    return jnp.max(
        chances.reshape(head_count, row_count // block_len, block_len, column_count), axis=2
    )


def key_pass(
    held_rows, query_pos, query_doc, key_shard, doc_ids, block_len, score_scale, total_blocks
):
    head_count, row_count, head_dim = held_rows.shape
    query_top = jnp.max(query_pos)
    doc_floor = jnp.min(query_doc)
    initial = (
        jnp.full((head_count, row_count, total_blocks), NEG_FILL, jnp.float32),
        jnp.full((head_count, row_count), NEG_FILL, jnp.float32),
        jnp.zeros((head_count, row_count), jnp.float32),
        jnp.zeros((total_blocks, 3 * head_dim), jnp.float32),
    )
    key_piece = lax.all_gather(key_shard, "ctx", axis=0, tiled=True)
    piece_rows = key_piece.shape[0]
    sub_rows = math.gcd(piece_rows, BLOCK_CAP)

    def advance(turn_index, inner):
        stats = inner[:3]
        pooled = inner[3]
        key_start = turn_index * sub_rows
        key_block = lax.dynamic_slice_in_dim(key_piece, turn_index * sub_rows, sub_rows, 0)
        pooled = lax.dynamic_update_slice_in_dim(
            pooled, pool_keys(key_block, block_len), key_start // block_len, 0
        )

        def sweep(current):
            return tile_update(
                current,
                held_rows,
                query_pos,
                query_doc,
                key_block,
                key_start,
                0,
                doc_ids,
                block_len,
                score_scale,
            )

        def keep_stats(current):
            return current

        last_doc = lax.dynamic_index_in_dim(
            doc_ids, (key_start + sub_rows - 1) // block_len, 0, keepdims=False
        )
        needed = (key_start <= query_top) & (last_doc >= doc_floor)
        stats = lax.cond(needed, sweep, keep_stats, stats)
        return stats + (pooled,)

    score_table, row_max, row_sum, pooled = lax.fori_loop(
        0, piece_rows // sub_rows, advance, initial
    )
    return (finish_maps(score_table, row_max, row_sum, block_len), pooled)


def gate_gradients(query_pool, pooled, gate_query, gate_key, block_map, block_allowed):
    query_gate = jnp.einsum(
        "hbd,hde->hbe", query_pool, gate_query.astype(jnp.float32), precision=lax.Precision.HIGHEST
    )
    key_gate = jnp.dot(pooled, gate_key.astype(jnp.float32), precision=lax.Precision.HIGHEST)
    gate_logits = jnp.einsum("hbe,ke->hbk", query_gate, key_gate, precision=lax.Precision.HIGHEST)
    gate_exp = jnp.where(block_allowed[None], jnp.exp(gate_logits), 0.0)
    gate_prob = gate_exp / jnp.sum(gate_exp, axis=2, keepdims=True)
    target = block_map / jnp.sum(block_map, axis=2, keepdims=True)
    diff = gate_prob - target
    query_back = jnp.einsum("hbk,ke->hbe", diff, key_gate, precision=lax.Precision.HIGHEST)
    query_term = jnp.einsum("hbd,hbe->hde", query_pool, query_back, precision=lax.Precision.HIGHEST)
    key_back = jnp.einsum("hbk,hbe->ke", diff, query_gate, precision=lax.Precision.HIGHEST)
    key_term = jnp.dot(pooled.T, key_back, precision=lax.Precision.HIGHEST)
    return (query_term, key_term)


def shards(queries, keys, doc_ids, gate_query, gate_key):
    head_count, row_count, head_dim = queries.shape
    block_len = BLK
    total_blocks = doc_ids.shape[0]
    score_scale = 1.0 / math.sqrt(head_dim)
    ctx_total = lax.axis_size("ctx")
    row_index = lax.axis_index("row")
    ctx_index = lax.axis_index("ctx")
    query_pos = held_positions(row_index, ctx_index, ctx_total, row_count)
    query_doc = block_docs(doc_ids, query_pos, block_len)
    held_maps, pooled = key_pass(
        queries, query_pos, query_doc, keys, doc_ids, block_len, score_scale, total_blocks
    )
    home_count = row_count // block_len
    home_blocks = (row_index * ctx_total + ctx_index) * home_count + jnp.arange(
        home_count, dtype=jnp.int32
    )
    home_docs = jnp.take(doc_ids, home_blocks)
    all_blocks = jnp.arange(total_blocks, dtype=jnp.int32)
    block_allowed = (all_blocks[None, :] <= home_blocks[:, None]) & (
        doc_ids[None, :] == home_docs[:, None]
    )
    query_pool = jnp.mean(
        queries.astype(jnp.float32).reshape(head_count, home_count, block_len, head_dim), axis=2
    )
    query_term, key_term = gate_gradients(
        query_pool, pooled, gate_query, gate_key, held_maps, block_allowed
    )
    grad_query, grad_key = lax.psum((query_term, key_term), ("row", "ctx"))
    return (held_maps, grad_query, grad_key)


def solution(mesh):
    in_specs = (P(None, ("row", "ctx"), None), P("ctx", None), P(), P(), P())
    out_specs = (P(None, ("row", "ctx"), None), P(), P())
    return jax.shard_map(shards, mesh=mesh, in_specs=in_specs, out_specs=out_specs, check_vma=False)
```

profile of v0, /device:TPU:0, one launch (start us, length us, event | category | flops | bytes accessed | tf_op | source)
XLA Modules:
  0.0 220.2 jit_solution(13385890775669702233)
XLA Ops:
  7.2 0.0 all-gather.2.cloned.1.call-start
  7.2 0.7 all-gather.2.cloned.1.call-update
  7.9 0.0 all-reduce.3.cloned.1.call-start
  8.0 0.1 pad_add_fusion
  8.1 0.1 reshape.164
  8.2 0.1 slice_reduce_fusion
  8.3 1.3 gather_fusion
  9.6 1.3 gather_fusion.1
  10.9 0.6 fusion.18
  12.9 0.7 broadcast_reduce_fusion
  13.6 0.1 compare_and_fusion.1
  13.7 0.2 fusion.12
  14.0 26.4 %all-gather.2.cloned.1.call-done = bf16[4096,128]{1,0:T(8,128)(2,1)} async-done(((bf16[1024,128]{1,0:T(8,128)(2,1)}), bf16[4096,128]{1,0:T(8,128)(2,1)}) %all-gather.2.cloned.1.call-update) | async-done | bytes 1048592 | tf_op jit(solution)/shard_map/all_gather | solution.py:92
  40.4 27.2 %while.25 = (s32[]{:T(128)}, f32[5,128,64]{1,2,0:T(8,128)S(1)}, f32[5,128]{1,0:T(8,128)S(1)}, f32[5,128]{1,0:T(8,128)S(1)}, f32[64,384]{1,0:T(8,128)S(1)}, /*ind...) while((s32[]{:T(128)}, f32[5,128,64]{1,2,0:T(8,128)S(1)}, ...), condition=%wide.region_12.14_spmd.clone, body=%wide.region_3.13_spmd.clone.sunk | while | flops 86640432 | bytes 7622712 | solution.py:129
  40.4 1.0 bitcast_reduce_fusion.4
  41.5 0.2 dynamic_update_slice.19
  41.7 0.6 dynamic_slice.37
  43.6 2.2 conditional.3
  43.6 0.1 dynamic_slice.29
  43.7 0.1 broadcast_in_dim.36
  43.7 0.1 eq.30
  43.8 0.1 broadcast_in_dim.76
  43.9 0.1 eq.32
  44.0 0.1 compare_and_fusion
  44.1 0.4 fusion.23
  44.6 0.4 select_reduce_fusion
  45.0 0.4 copy.26
  45.4 0.2 bitcast_reduce_fusion
  45.6 0.1 dynamic_update_slice.15
  45.8 0.9 bitcast_reduce_fusion.4
  46.8 0.2 dynamic_update_slice.19
  47.0 0.6 dynamic_slice.37
  48.9 0.9 bitcast_reduce_fusion.4
  49.9 0.2 dynamic_update_slice.19
  50.2 0.6 dynamic_slice.37
  52.0 0.9 bitcast_reduce_fusion.4
  53.1 0.2 dynamic_update_slice.19
  53.3 0.6 dynamic_slice.37
  55.1 0.9 bitcast_reduce_fusion.4
  56.2 0.2 dynamic_update_slice.19
  56.4 0.6 dynamic_slice.37
  58.3 0.9 bitcast_reduce_fusion.4
  59.3 0.2 dynamic_update_slice.19
  59.5 0.6 dynamic_slice.37
  61.4 0.9 bitcast_reduce_fusion.4
  62.5 0.2 dynamic_update_slice.19
  62.7 0.6 dynamic_slice.37
  64.5 0.9 bitcast_reduce_fusion.4
  65.6 0.1 dynamic_update_slice.19
  65.8 0.6 dynamic_slice.37
  67.7 0.2 copy.33
  67.9 0.1 reduce_sum.58
  68.0 0.1 copy.29
  68.1 0.2 convolution_bitcast_fusion.1
  68.3 0.2 fusion.4
  68.4 0.2 fusion.10
  68.6 0.3 convolution_bitcast_fusion
  69.0 0.2 fusion.21
  69.2 1.2 fusion.24
  70.4 1.4 fusion.8
  71.8 0.0 all-reduce.3.cloned.1.call-update
  71.8 138.2 %all-reduce.3.cloned.1.call-done = (f32[5,128,128]{2,1,0:T(8,128)}, f32[384,128]{1,0:T(8,128)}) async-done(((f32[5,128,128]{2,1,0:T(8,128)}, f32[384,128]{1,0:T(8,128)}), (f32[5,128,128]{2,1,0:T(8,128)}, f32[384,128]{1,0:T(8,128)})) %all-reduce.3.cloned.1.call-update) | async-done | bytes 524304 | tf_op jit(solution)/shard_map/psum | solution.py:180
  210.1 1.7 copy.70
  211.8 1.6 copy.71
  (68 shorter events, 0.8 us)
Async XLA Ops:
  7.2 6.6 %copy-start = (bf16[5,128,128]{2,1,0:T(8,128)(2,1)S(1)}, bf16[5,128,128]{2,1,0:T(8,128)(2,1)}, u32[]{:S(2)}) copy-start(bf16[5,128,128]{2,1,0:T(8,128)(2,1)} %param.14) | copy-start | bytes 491524
  7.2 6.5 %copy-start.1 = (s32[64]{0:T(128)S(1)}, s32[64]{0:T(128)}, u32[]{:S(2)}) copy-start(s32[64]{0:T(128)} %param.13) | copy-start | bytes 772
  7.2 6.4 %copy-start.2 = (bf16[5,128,128]{2,1,0:T(8,128)(2,1)S(1)}, bf16[5,128,128]{2,1,0:T(8,128)(2,1)}, u32[]{:S(2)}) copy-start(bf16[5,128,128]{2,1,0:T(8,128)(2,1)} %param.11) | copy-start | bytes 491524
  7.2 33.2 %all-gather.2.cloned.1.call-start = ((), (), s32[]{:S(2)}) async-start(), calls=%async_computation | async-start | bytes 1310720 | tf_op jit(solution)/shard_map/all_gather | solution.py:92
  7.9 202.1 %all-reduce.3.cloned.1.call-start = ((), (), s32[]{:S(2)}) async-start(), calls=%async_computation.1 | async-start | bytes 1048576 | tf_op jit(solution)/shard_map/psum | solution.py:180
  40.4 27.7 %copy-start.3 = (bf16[384,128]{1,0:T(8,128)(2,1)S(1)}, bf16[384,128]{1,0:T(8,128)(2,1)}, u32[]{:S(2)}) copy-start(bf16[384,128]{1,0:T(8,128)(2,1)} %param.15) | copy-start | bytes 294916
  67.9 145.5 %copy-start.4 = (f32[5,2,64]{2,1,0:T(2,128)}, f32[5,2,64]{2,1,0:T(2,128)S(1)}, u32[]{:S(2)}) copy-start(f32[5,2,64]{2,1,0:T(2,128)S(1)} %bitcast_reduce_fusion.2) | copy-start | bytes 7684
Sparse Core Ops, SparseCore 0:
  9.6 30.7 all-gather.1
  71.9 138.0 all-reduce.2
where the time goes:
time: 221 us; the launch traced here: 220 us
  waiting for transfers between devices  165 us (75%)
  between operations  15.5 us (7%)
  local copies, waits for them, and re-layouts  13.4 us (6%)
  loops' own time  11 us (5%)
  other arithmetic  10.7 us (5%)
  matrix products  4.21 us (2%)
    psum x1, waiting for transfers between devices, shards(): grad_query, grad_key = lax.psum((query_term, key_term), ('row', 'ctx'))  138 us
    all_gather x1, waiting for transfers between devices, key_pass(): key_piece = lax.all_gather(key_shard, 'ctx', axis=0, tiled=True)  26.4 us
    another operation x1, loops' own time, key_pass(): lax.fori_loop(0, piece_rows // sub_rows, advance, initial)  10.8 us
    reduce_max x16, other arithmetic, pool_keys(): jnp.max(grouped, axis=1)  7.65 us
    dynamic_slice x8, local copies, waits for them, and re-layouts, advance(): lax.dynamic_index_in_dim(doc_ids, (key_start + sub_rows - 1) // block_len...  4.69 us
  transfers between devices with their start and end apart: 2, of which 2 were waited for; matrix products, arithmetic and copies ran while one was open for 2% of the time, Pallas kernels for 0%

commit v1 on v0

--- a/solution.py
+++ b/solution.py
@@ -7,6 +7,12 @@
 BLK = 64
 NEG_FILL = -1e30
 BLOCK_CAP = 512
+
+
+def laid_out(blocks, dim):
+    blocks = jnp.moveaxis(blocks, 0, dim)
+    shape = blocks.shape
+    return blocks.reshape(*shape[:dim], shape[dim] * shape[dim + 1], *shape[dim + 2 :])
 
 
 def pool_keys(key_block, block_len):
@@ -89,7 +95,19 @@
         jnp.zeros((head_count, row_count), jnp.float32),
         jnp.zeros((total_blocks, 3 * head_dim), jnp.float32),
     )
-    key_piece = lax.all_gather(key_shard, "ctx", axis=0, tiled=True)
+    devices = lax.axis_size("ctx")
+    pairs = [(i, (i + 1) % devices) for i in range(devices)]
+    back = [(b, a) for a, b in pairs]
+    lower, upper = ([], [])
+    for step in range(devices - 1):
+        if step % 2 == 0:
+            lower.append(lax.ppermute(lower[-1] if lower else key_shard, "ctx", pairs))
+        else:
+            upper.append(lax.ppermute(upper[-1] if upper else key_shard, "ctx", back))
+    parts = jnp.stack([*lower[::-1], key_shard, *upper])
+    shift = lax.axis_index("ctx") - len(lower)
+    parts = parts[(jnp.arange(devices) - shift) % devices]
+    key_piece = laid_out(parts, 0)
     piece_rows = key_piece.shape[0]
     sub_rows = math.gcd(piece_rows, BLOCK_CAP)
 

time: 221 us -> 211 us (0.955)
  waiting for transfers between devices: 165 us -> 147 us
  starting transfers between devices: 0.08 us -> 5.24 us
    all_gather x1 -> x0, waiting for transfers between devices: 26.4 us -> none  [key_pass(): key_piece = lax.all_gather(key_shard, 'ctx', axis=0, tiled=True)]
    ppermute x0 -> x3, waiting for transfers between devices: none -> 10.1 us  [the longest x2 7.9 us: key_pass(): lower.append(lax.ppermute(lower[-1] if lower else key_shard, 'ctx', pairs))]
    ppermute x0 -> x3, starting transfers between devices: none -> 5.2 us  [the longest x2 3.11 us: key_pass(): lower.append(lax.ppermute(lower[-1] if lower else key_shard, 'ctx', pairs))]
  transfers between devices with their start and end apart: 2 -> 4, of which waited for: 2 -> 4; matrix products, arithmetic and copies ran while one was open for 2% -> 3% of each run, Pallas kernels for 0% -> 0%
where the time goes in v1:
time: 211 us; the launch traced here: 210 us
  waiting for transfers between devices  147 us (70%)
  between operations  15.5 us (7%)
  local copies, waits for them, and re-layouts  15.1 us (7%)
  other arithmetic  12.5 us (6%)
  loops' own time  11.3 us (5%)
  starting transfers between devices  5.24 us (2%)
  matrix products  4.21 us (2%)
    psum x1, waiting for transfers between devices, shards(): grad_query, grad_key = lax.psum((query_term, key_term), ('row', 'ctx'))  136 us
    another operation x1, loops' own time, key_pass(): lax.fori_loop(0, piece_rows // sub_rows, advance, initial)  11.1 us
    ppermute x2, waiting for transfers between devices, key_pass(): lower.append(lax.ppermute(lower[-1] if lower else key_shard, 'ctx', pairs))  7.9 us
    reduce_max x16, other arithmetic, pool_keys(): jnp.max(grouped, axis=1)  7.65 us
    dynamic_slice x8, local copies, waits for them, and re-layouts, advance(): lax.dynamic_index_in_dim(doc_ids, (key_start + sub_rows - 1) // block_len...  4.69 us
  transfers between devices with their start and end apart: 4, of which 4 were waited for; matrix products, arithmetic and copies ran while one was open for 3% of the time, Pallas kernels for 0%

profile of v1, /device:TPU:0, one launch (start us, length us, event | category | flops | bytes accessed | tf_op | source)
XLA Modules:
  0.0 210.5 jit_solution(4041804967353970041)
XLA Ops:
  7.2 3.1 %collective-permute-start = (bf16[1024,128]{1,0:T(8,128)(2,1)}, bf16[1024,128]{1,0:T(8,128)(2,1)S(1)}, u32[]{:S(2)}, u32[]{:S(2)}) collective-permute-start(bf16[1024,128]{1,0:T(8,128)(2,1)} %param.12), channel_id=1, source_target_pairs={{0,1},{1,2},{2,3},{3,0},{4,5},{5,6},{6,7},{7,4},{8,9},{9,10},{10,1... | collective-permute-start | bytes 786440 | tf_op jit(solution)/shard_map/ppermute | solution.py:104
  10.3 2.1 collective-permute-start.2
  12.4 0.1 pad_add_fusion
  12.5 0.1 reshape.216
  12.6 0.1 slice_reduce_fusion
  12.7 1.3 gather_fusion.1
  14.1 0.8 broadcast_reduce_fusion
  14.8 1.3 gather_fusion.2
  16.2 1.0 convert_reduce_fusion.2
  17.1 0.7 compare_and_fusion.1
  17.9 1.9 collective-permute-done
  19.8 0.6 fusion.20
  21.7 0.2 fusion.12
  22.0 2.2 %collective-permute-done.2 = bf16[1024,128]{1,0:T(8,128)(2,1)S(1)} collective-permute-done((bf16[1024,128]{1,0:T(8,128)(2,1)}, bf16[1024,128]{1,0:T(8,128)(2,1)S(1)}, u32[]{:S(2)}, u32[]{:S(2)}) %collective-permute-start.2) | collective-permute-done | bytes 262176 | tf_op jit(solution)/shard_map/ppermute | solution.py:106
  24.2 6.0 %collective-permute-done.1 = bf16[1024,128]{1,0:T(8,128)(2,1)S(1)} collective-permute-done((bf16[1024,128]{1,0:T(8,128)(2,1)S(1)}, bf16[1024,128]{1,0:T(8,128)(2,1)S(1)}, u32[]{:S(2)}, u32[]{:S(2)}) %collective-permute-start.1) | collective-permute-done | bytes 262176 | tf_op jit(solution)/shard_map/ppermute | solution.py:104
  30.2 0.1 pad_maximum_fusion.1
  30.3 1.7 gather_fusion
  32.1 27.5 %while.25 = (s32[]{:T(128)}, f32[5,128,64]{1,2,0:T(8,128)S(1)}, f32[5,128]{1,0:T(8,128)S(1)}, f32[5,128]{1,0:T(8,128)S(1)}, f32[64,384]{1,0:T(8,128)S(1)}, /*ind...) while((s32[]{:T(128)}, f32[5,128,64]{1,2,0:T(8,128)S(1)}, ...), condition=%wide.region_12.14_spmd.clone, body=%wide.region_3.13_spmd.clone.sunk | while | flops 86640432 | bytes 7622712 | solution.py:147
  32.1 1.0 bitcast_reduce_fusion.4
  33.2 0.2 dynamic_update_slice.19
  33.4 0.6 dynamic_slice.37
  35.3 2.2 %conditional.3 = ((f32[5,128,64]{1,2,0:T(8,128)S(1)}, f32[5,128]{1,0:T(8,128)S(1)}, f32[5,128]{1,0:T(8,128)S(1)})) conditional(s32[]{:T(128)} %convert_element_type.31, (f32[5,128,64]{1,2,0:T(8,128)S(1)}, f32[5,128]{1,0:T(8,128)S(1)}, f32[5,128]{1,0:T(8,128)S(1)}) %tuple.78, (s32[]{:T(128)}, s32[128]{0:T(128)S(1)}, s32[64]{0:T(128)S(1)}, ...), branch_computations={%region_4.5_spmd, %region_5.9_spmd} | conditional | flops 86373136 | bytes 7155020 | solution.py:144
  35.4 0.1 eq.32
  35.6 0.1 eq.34
  35.7 0.1 compare_and_fusion
  35.8 0.4 fusion.25
  36.3 0.4 select_reduce_fusion
  36.7 0.4 copy.26
  37.1 0.2 bitcast_reduce_fusion
  37.3 0.1 dynamic_update_slice.15
  37.5 0.9 bitcast_reduce_fusion.4
  38.5 0.2 dynamic_update_slice.19
  38.7 0.6 dynamic_slice.37
  40.6 0.9 bitcast_reduce_fusion.4
  41.7 0.2 dynamic_update_slice.19
  41.9 0.6 dynamic_slice.37
  43.8 0.9 bitcast_reduce_fusion.4
  44.9 0.2 dynamic_update_slice.19
  45.1 0.6 dynamic_slice.37
  47.0 0.9 bitcast_reduce_fusion.4
  48.0 0.2 dynamic_update_slice.19
  48.2 0.6 dynamic_slice.37
  50.1 0.9 bitcast_reduce_fusion.4
  51.2 0.2 dynamic_update_slice.19
  51.4 0.6 dynamic_slice.37
  53.3 0.9 bitcast_reduce_fusion.4
  54.4 0.2 dynamic_update_slice.19
  54.6 0.6 dynamic_slice.37
  56.5 0.9 bitcast_reduce_fusion.4
  57.5 0.1 dynamic_update_slice.19
  57.7 0.6 dynamic_slice.37
  59.6 0.2 copy.33
  59.9 0.1 reduce_sum.58
  60.0 0.1 copy.29
  60.1 0.2 convolution_bitcast_fusion.1
  60.3 0.2 fusion.4
  60.4 0.2 fusion.10
  60.6 0.3 convolution_bitcast_fusion
  61.0 0.2 fusion.23
  61.2 1.2 fusion.26
  62.4 1.4 fusion.8
  63.8 136.5 %all-reduce.3.cloned.1.call-done = (f32[5,128,128]{2,1,0:T(8,128)}, f32[384,128]{1,0:T(8,128)}) async-done(((f32[5,128,128]{2,1,0:T(8,128)}, f32[384,128]{1,0:T(8,128)}), (f32[5,128,128]{2,1,0:T(8,128)}, f32[384,128]{1,0:T(8,128)})) %all-reduce.3.cloned.1.call-update) | async-done | bytes 524304 | tf_op jit(solution)/shard_map/psum | solution.py:198
  200.3 1.7 copy.70
  202.0 1.6 copy.71
  (77 shorter events, 1.0 us)
Async XLA Ops:
  7.2 14.6 %copy-start = (bf16[5,128,128]{2,1,0:T(8,128)(2,1)S(1)}, bf16[5,128,128]{2,1,0:T(8,128)(2,1)}, u32[]{:S(2)}) copy-start(bf16[5,128,128]{2,1,0:T(8,128)(2,1)} %param.14) | copy-start | bytes 491524
  7.2 23.0 %copy-start.3 = (bf16[1024,128]{1,0:T(8,128)(2,1)S(1)}, bf16[1024,128]{1,0:T(8,128)(2,1)}, u32[]{:S(2)}) copy-start(bf16[1024,128]{1,0:T(8,128)(2,1)} %param.12) | copy-start | bytes 786436
  7.2 193.1 %all-reduce.3.cloned.1.call-start = ((), (), s32[]{:S(2)}) async-start(), calls=%async_computation | async-start | bytes 1048576 | tf_op jit(solution)/shard_map/psum | solution.py:198
  7.2 12.5 %collective-permute-start = (bf16[1024,128]{1,0:T(8,128)(2,1)}, bf16[1024,128]{1,0:T(8,128)(2,1)S(1)}, u32[]{:S(2)}, u32[]{:S(2)}) collective-permute-start(bf16[1024,128]{1,0:T(8,128)(2,1)} %param.12), channel_id=1, source_target_pairs={{0,1},{1,2},{2,3},{3,0},{4,5},{5,6},{6,7},{7,4},{8,9},{9,10},{10,1... | collective-permute-start | bytes 786440 | tf_op jit(solution)/shard_map/ppermute | solution.py:104
  10.3 13.8 %collective-permute-start.2 = (bf16[1024,128]{1,0:T(8,128)(2,1)}, bf16[1024,128]{1,0:T(8,128)(2,1)S(1)}, u32[]{:S(2)}, u32[]{:S(2)}) collective-permute-start(bf16[1024,128]{1,0:T(8,128)(2,1)} %param.12), channel_id=1, source_target_pairs={{1,0},{2,1},{3,2},{0,3},{5,4},{6,5},{7,6},{4,7},{9,8},{10,9},{11,1... | collective-permute-start | bytes 786440 | tf_op jit(solution)/shard_map/ppermute | solution.py:106
  19.8 10.4 %collective-permute-start.1 = (bf16[1024,128]{1,0:T(8,128)(2,1)S(1)}, bf16[1024,128]{1,0:T(8,128)(2,1)S(1)}, u32[]{:S(2)}, u32[]{:S(2)}) collective-permute-start(bf16[1024,128]{1,0:T(8,128)(2,1)S(1)} %collective-permute-done), channel_id=1, source_target_pairs={{0,1},{1,2},{2,3},{3,0},{4,5},{5,6},{6,7},{7,4},{8,9},{9,10},{10,1... | collective-permute-start | bytes 786440 | tf_op jit(solution)/shard_map/ppermute | solution.py:104
  30.3 1.7 copy-start.1
  30.3 1.7 copy-start.2
  32.1 28.0 %copy-start.4 = (bf16[384,128]{1,0:T(8,128)(2,1)S(1)}, bf16[384,128]{1,0:T(8,128)(2,1)}, u32[]{:S(2)}) copy-start(bf16[384,128]{1,0:T(8,128)(2,1)} %param.15) | copy-start | bytes 294916
  59.9 143.8 %copy-start.5 = (f32[5,2,64]{2,1,0:T(2,128)}, f32[5,2,64]{2,1,0:T(2,128)S(1)}, u32[]{:S(2)}) copy-start(f32[5,2,64]{2,1,0:T(2,128)S(1)} %bitcast_reduce_fusion.2) | copy-start | bytes 7684
Sparse Core Ops, SparseCore 0:
  63.9 136.3 all-reduce.2
